TPU v7x, 32 devices: a whole 2x2x4 slice. The times are simulated.
32 devices in a mesh: grp: 4 (over x, core), ctx: 4 (over z), wt: 2 (over y).
Axes of the slice: x: 2, y: 2, z: 4, core: 2. Of those that a mesh axis runs over, the one named last changes fastest.
Arguments:
- tokens: bfloat16 [8, 2048, 1280], P(('grp', 'wt'), 'ctx'), may hold values from -6 to 6
- segments: int32 [8, 2048], P(('grp', 'wt')), may hold values from 0 to 2, as said below
- w_qkv: bfloat16 [1280, 3840], P('wt'), may hold values from -0.15625 to 0.15625
- w_proj: bfloat16 [1280, 1280], P('wt'), may hold values from -1.25 to 1.25
- w_in: bfloat16 [1280, 1280], P('wt'), may hold values from -0.15625 to 0.15625
- w_out: bfloat16 [1280, 1280], P('wt'), may hold values from -0.15625 to 0.15625
- gain_attn: float32 [1280], replicated, may hold values from 0.5 to 1.5
- gain_mlp: float32 [1280], replicated, may hold values from 0.5 to 1.5
- query_scale: float32 [80], replicated, may hold values from -0.5 to 1.5
- cotangent: bfloat16 [8, 2048, 1280], P(('grp', 'wt'), 'ctx'), may hold values from -6 to 6
Outputs:
- layer_out: bfloat16 [8, 2048, 1280], P(('grp', 'wt'), 'ctx')
- grad_tokens: bfloat16 [8, 2048, 1280], P(('grp', 'wt'), 'ctx')
- grad_w_qkv: float32 [1280, 3840], P('wt')
- grad_w_proj: float32 [1280, 1280], P('wt')
- grad_w_in: float32 [1280, 1280], P('wt')
- grad_w_out: float32 [1280, 1280], P('wt')
- grad_gain_attn: float32 [1280], replicated
- grad_gain_mlp: float32 [1280], replicated
- grad_query_scale: float32 [80], replicated
Inputs may be any that keep to these rules, and one draw needn't show every extreme that they name: `segments`: in each group the id starts at 0, never falls, and every id of 0 to 2 is used. Segment 0 ends 1024 - r tokens into the group, r below 256; each later continuation starts 512 + j tokens after the one before, j within 128 either way; the last runs to the group's end.
All inputs are finite; a program needn't handle non-finite values.
Results may differ from a plain program's by a relative error of at most 0.02.
Values may be sent and summed in bfloat16 or wider, within the bound.
No kernel may reach another device: no remote copies, remote signals or barrier semaphores. Data moves between devices by JAX's collectives and lax.ppermute only.
A program may use at most 256 MiB of HBM per device.

v0:
```python
import math
import jax
import jax.numpy as jnp
from jax import lax
from jax.sharding import PartitionSpec as P

D = 1280
H = 16
HD = 80
epsilon = 1e-06
scale_base = 1.442695041
masked_fill = -1e30


def rms_inverse(values):
    return lax.rsqrt(jnp.mean(values * values, axis=-1, keepdims=True) + epsilon)


def norm_back(values, inverse, grad_scaled):
    return inverse * grad_scaled - values * (inverse * inverse * inverse) * jnp.mean(
        grad_scaled * values, axis=-1, keepdims=True
    )


def times_trans(left, right):
    return lax.dot_general(
        left, right, (((1,), (1,)), ((), ())), preferred_element_type=jnp.float32
    )


def trans_times(left, right):
    return lax.dot_general(
        left, right, (((0,), (0,)), ((), ())), preferred_element_type=jnp.float32
    )


def visible(query_pos, query_seg, seg_row, offset, key_count):
    key_pos = offset + jnp.arange(key_count, dtype=jnp.int32)
    key_seg = lax.dynamic_slice_in_dim(seg_row, offset, key_count)
    return (key_pos[None, :] <= query_pos[:, None]) & (
        (key_seg[None, :] == 0) | (key_seg[None, :] == query_seg[:, None])
    )


def blocked(step_fn, carried, shard_rows):
    length = shard_rows.shape[0]
    width = math.gcd(length, 512)

    def advance(counter, carried_in):
        beginning = counter * width
        subrows = lax.dynamic_slice_in_dim(shard_rows, beginning, width, 0)
        return step_fn(carried_in, subrows, beginning)

    return lax.fori_loop(0, length // width, advance, carried)


def local(
    tokens, segments, w_qkv, w_proj, w_in, w_out, gain_attn, gain_mlp, query_scale, cotangent
):
    inputs = tokens[0].astype(jnp.float32)
    rows = inputs.shape[0]
    seg_row = segments[0]
    group_len = seg_row.shape[0]
    own_index = lax.axis_index("ctx")
    own_offset = own_index * rows
    query_pos = own_offset + jnp.arange(rows, dtype=jnp.int32)
    query_seg = lax.dynamic_slice_in_dim(seg_row, own_offset, rows)
    full_qkv, full_proj, full_in, full_out = (
        lax.all_gather(w_qkv, "wt", axis=0, tiled=True),
        lax.all_gather(w_proj, "wt", axis=0, tiled=True),
        lax.all_gather(w_in, "wt", axis=0, tiled=True),
        lax.all_gather(w_out, "wt", axis=0, tiled=True),
    )
    inverse_attn = rms_inverse(inputs)
    normed = (inputs * inverse_attn * gain_attn).astype(jnp.bfloat16)
    project = jnp.dot(normed, full_qkv, preferred_element_type=jnp.float32)
    dim_scale = scale_base / math.sqrt(HD) * jax.nn.softplus(query_scale)
    raw_queries = project[:, :D].reshape(rows, H, HD)
    queries = (raw_queries * dim_scale).astype(jnp.bfloat16)
    keyval = project[:, D:].astype(jnp.bfloat16)

    def forward_step(carried, subrows, offset):
        running_max, running_sum, accum = carried
        key_count = subrows.shape[0]
        keys_part = subrows[:, :D].reshape(key_count, H, HD)
        values_part = subrows[:, D:].reshape(key_count, H, HD)
        scores = jnp.einsum("qhd,khd->hqk", queries, keys_part, preferred_element_type=jnp.float32)
        allowed = visible(query_pos, query_seg, seg_row, offset, key_count)[None]
        masked = jnp.where(allowed, scores, masked_fill)
        new_max = jnp.maximum(running_max, jnp.max(masked, axis=-1))
        factor = jnp.exp(running_max - new_max)
        exponent = jnp.where(allowed, jnp.exp(masked - new_max[:, :, None]), 0.0)
        running_sum = running_sum * factor + jnp.sum(exponent, axis=-1)
        accum = accum * jnp.transpose(factor)[:, :, None] + jnp.einsum(
            "hqk,khd->qhd",
            exponent.astype(jnp.bfloat16),
            values_part,
            preferred_element_type=jnp.float32,
        )
        return (new_max, running_sum, accum)

    start_state = (
        jnp.full((H, rows), masked_fill, jnp.float32),
        jnp.zeros((H, rows), jnp.float32),
        jnp.zeros((rows, H, HD), jnp.float32),
    )
    running_max, running_sum, accum = blocked(
        forward_step, start_state, lax.all_gather(keyval, "ctx", axis=0, tiled=True)
    )
    logsum = running_max + jnp.log(running_sum)
    attn_float = accum / jnp.transpose(running_sum)[:, :, None]
    attended = attn_float.reshape(rows, D).astype(jnp.bfloat16)
    resid = inputs + jnp.dot(attended, full_proj, preferred_element_type=jnp.float32)
    inverse_mlp = rms_inverse(resid)
    normed_mlp = (resid * inverse_mlp * gain_mlp).astype(jnp.bfloat16)
    hidden = jnp.dot(normed_mlp, full_in, preferred_element_type=jnp.float32)
    active = jax.nn.silu(hidden).astype(jnp.bfloat16)
    layer_out = (resid + jnp.dot(active, full_out, preferred_element_type=jnp.float32)).astype(
        jnp.bfloat16
    )
    back_qkv, back_proj, back_in, back_out = (
        lax.all_gather(w_qkv, "wt", axis=0, tiled=True),
        lax.all_gather(w_proj, "wt", axis=0, tiled=True),
        lax.all_gather(w_in, "wt", axis=0, tiled=True),
        lax.all_gather(w_out, "wt", axis=0, tiled=True),
    )
    grad_out = cotangent[0].astype(jnp.float32)
    grad_mlp = cotangent[0]
    grad_active = times_trans(grad_mlp, back_out)
    grad_w_out = trans_times(active, grad_mlp)
    sigmoid_h = jax.nn.sigmoid(hidden)
    grad_hidden = (grad_active * sigmoid_h * (1.0 + hidden * (1.0 - sigmoid_h))).astype(
        jnp.bfloat16
    )
    grad_w_in = trans_times(normed_mlp, grad_hidden)
    grad_normed_mlp = times_trans(grad_hidden, back_in)
    grad_gain_mlp = jnp.sum(grad_normed_mlp * resid * inverse_mlp, axis=0)
    grad_resid = grad_out + norm_back(resid, inverse_mlp, grad_normed_mlp * gain_mlp)
    grad_proj = grad_resid.astype(jnp.bfloat16)
    grad_w_proj = trans_times(attended, grad_proj)
    grad_attended = times_trans(grad_proj, back_proj).astype(jnp.bfloat16).reshape(rows, H, HD)
    delta = jnp.transpose(jnp.sum(grad_attended.astype(jnp.float32) * attn_float, axis=-1))

    def backward_step(carried, subrows, offset):
        grad_queries, grad_keyval = carried
        key_count = subrows.shape[0]
        keys_part = subrows[:, :D].reshape(key_count, H, HD)
        values_part = subrows[:, D:].reshape(key_count, H, HD)
        scores = jnp.einsum("qhd,khd->hqk", queries, keys_part, preferred_element_type=jnp.float32)
        allowed = visible(query_pos, query_seg, seg_row, offset, key_count)[None]
        probs = jnp.where(
            allowed, jnp.exp(jnp.where(allowed, scores, masked_fill) - logsum[:, :, None]), 0.0
        )
        grad_probs = jnp.einsum(
            "qhd,khd->hqk", grad_attended, values_part, preferred_element_type=jnp.float32
        )
        grad_scores = (probs * (grad_probs - delta[:, :, None])).astype(jnp.bfloat16)
        grad_queries = grad_queries + jnp.einsum(
            "hqk,khd->qhd", grad_scores, keys_part, preferred_element_type=jnp.float32
        )
        grad_keys = jnp.einsum(
            "hqk,qhd->khd", grad_scores, queries, preferred_element_type=jnp.float32
        )
        grad_values = jnp.einsum(
            "hqk,qhd->khd",
            probs.astype(jnp.bfloat16),
            grad_attended,
            preferred_element_type=jnp.float32,
        )
        combined = jnp.concatenate(
            [grad_keys.reshape(key_count, D), grad_values.reshape(key_count, D)], axis=1
        )
        current = lax.dynamic_slice_in_dim(grad_keyval, offset, key_count, 0)
        grad_keyval = lax.dynamic_update_slice_in_dim(grad_keyval, current + combined, offset, 0)
        return (grad_queries, grad_keyval)

    back_state = (jnp.zeros((rows, H, HD), jnp.float32), jnp.zeros((group_len, 2 * D), jnp.float32))
    grad_queries, grad_keyval = blocked(
        backward_step, back_state, lax.all_gather(keyval, "ctx", axis=0, tiled=True)
    )
    grad_keyval_own = lax.psum_scatter(
        grad_keyval.astype(jnp.bfloat16), "ctx", scatter_dimension=0, tiled=True
    ).astype(jnp.float32)
    grad_dims = jnp.sum(grad_queries * raw_queries, axis=(0, 1))
    grad_query_scale = grad_dims * (scale_base / math.sqrt(HD)) * jax.nn.sigmoid(query_scale)
    grad_project = jnp.concatenate(
        [(grad_queries * dim_scale).reshape(rows, D), grad_keyval_own], axis=1
    ).astype(jnp.bfloat16)
    grad_w_qkv = trans_times(normed, grad_project)
    grad_normed = times_trans(grad_project, back_qkv)
    grad_gain_attn = jnp.sum(grad_normed * inputs * inverse_attn, axis=0)
    grad_tokens = (grad_resid + norm_back(inputs, inverse_attn, grad_normed * gain_attn)).astype(
        jnp.bfloat16
    )
    shard_qkv, shard_proj, shard_in, shard_out = (
        lax.psum_scatter(
            grad_w_qkv.astype(jnp.bfloat16), "wt", scatter_dimension=0, tiled=True
        ).astype(jnp.float32),
        lax.psum_scatter(
            grad_w_proj.astype(jnp.bfloat16), "wt", scatter_dimension=0, tiled=True
        ).astype(jnp.float32),
        lax.psum_scatter(
            grad_w_in.astype(jnp.bfloat16), "wt", scatter_dimension=0, tiled=True
        ).astype(jnp.float32),
        lax.psum_scatter(
            grad_w_out.astype(jnp.bfloat16), "wt", scatter_dimension=0, tiled=True
        ).astype(jnp.float32),
    )
    total_qkv, total_proj, total_in, total_out = (
        lax.psum(shard_qkv.astype(jnp.bfloat16), ("grp", "ctx")).astype(jnp.float32),
        lax.psum(shard_proj.astype(jnp.bfloat16), ("grp", "ctx")).astype(jnp.float32),
        lax.psum(shard_in.astype(jnp.bfloat16), ("grp", "ctx")).astype(jnp.float32),
        lax.psum(shard_out.astype(jnp.bfloat16), ("grp", "ctx")).astype(jnp.float32),
    )
    total_gain_attn, total_gain_mlp, total_scale = lax.psum(
        (grad_gain_attn, grad_gain_mlp, grad_query_scale), ("grp", "ctx", "wt")
    )
    return (
        layer_out[None],
        grad_tokens[None],
        total_qkv,
        total_proj,
        total_in,
        total_out,
        total_gain_attn,
        total_gain_mlp,
        total_scale,
    )


def solution(mesh):
    placed = (
        P(("grp", "wt"), "ctx", None),
        P(("grp", "wt"), None),
        P("wt", None),
        P("wt", None),
        P("wt", None),
        P("wt", None),
        P(),
        P(),
        P(),
        P(("grp", "wt"), "ctx", None),
    )
    return jax.shard_map(
        local,
        mesh=mesh,
        in_specs=placed,
        out_specs=(
            P(("grp", "wt"), "ctx", None),
            P(("grp", "wt"), "ctx", None),
            P("wt", None),
            P("wt", None),
            P("wt", None),
            P("wt", None),
            P(),
            P(),
            P(),
        ),
        check_vma=False,
    )
```

profile of v0, /device:TPU:0, one launch (start us, length us, event | category | flops | bytes accessed | tf_op | source)
XLA Modules:
  0.0 1364.7 jit_solution(8203904737533730321)
XLA Ops:
  9.4 125.2 %all-gather.6.cloned.1.call-done = bf16[1280,3840]{1,0:T(8,128)(2,1)} async-done(((bf16[640,3840]{1,0:T(8,128)(2,1)}), bf16[1280,3840]{1,0:T(8,128)(2,1)}) %all-gather.6.cloned.1.call-update) | async-done | bytes 9830416 | tf_op jit(solution)/shard_map/all_gather | solution.py:69
  156.0 175.5 %all-gather.8.cloned.1.call-done = bf16[2048,2560]{1,0:T(8,128)(2,1)} async-done(((bf16[512,2560]{1,0:T(8,128)(2,1)}), bf16[2048,2560]{1,0:T(8,128)(2,1)}) %all-gather.8.cloned.1.call-update) | async-done | bytes 10485776 | tf_op jit(solution)/shard_map/all_gather | solution.py:108
  331.5 14.6 %copy.34 = bf16[2048,2560]{0,1:T(8,128)(2,1)} copy(bf16[2048,2560]{1,0:T(8,128)(2,1)} %all-gather.8.cloned.1.call-done) | data formatting | bytes 20971520
  346.1 122.1 %while.34 = (s32[]{:T(128)}, f32[16,512]{1,0:T(8,128)S(1)}, f32[16,512]{1,0:T(8,128)S(1)}, f32[512,16,80]{0,2,1:T(8,128)}, s32[2048]{0:T(1024)S(1)}, /*index=5*/...) while((s32[]{:T(128)}, f32[16,512]{1,0:T(8,128)S(1)}, ...), condition=%wide.region_4.5_spmd.clone, body=%wide.region_1.4_spmd.clone.sunk | while | flops 1387185664 | bytes 66340068 | solution.py:54
  356.6 9.2 fusion.115
  365.8 9.7 bitcast_add_fusion.4
  386.8 10.0 fusion.115
  396.7 10.4 bitcast_add_fusion.4
  417.8 9.2 fusion.115
  427.0 10.7 bitcast_add_fusion.4
  448.4 9.2 fusion.115
  457.5 10.4 bitcast_add_fusion.4
  500.7 9.7 broadcast_in_dim.141
  510.4 188.2 %while.35 = (s32[]{:T(128)}, f32[512,16,80]{0,2,1:T(8,128)}, f32[2048,2560]{0,1:T(8,128)}, bf16[2048,2560]{0,1:T(8,128)(2,1)}, s32[2048]{0:T(1024)S(1)}, /*index...) while((s32[]{:T(128)}, f32[512,16,80]{0,2,1:T(8,128)}, ...), condition=%wide.region_9.10_spmd.clone, body=%wide.region_8.9_spmd.clone.sunk | while | flops 3402368512 | bytes 138003792 | solution.py:54
  523.4 11.4 fusion.130
  534.8 9.7 fusion.129
  569.0 11.4 fusion.130
  580.4 9.7 fusion.129
  616.4 11.4 fusion.130
  627.8 9.7 fusion.129
  663.7 11.4 fusion.130
  675.1 9.7 fusion.129
  698.6 12.3 convert_element_type.118
  736.2 151.1 %reduce-scatter.6.cloned.1.call-done = bf16[512,2560]{0,1:T(8,128)(2,1)} async-done(((bf16[2048,2560]{0,1:T(8,128)(2,1)}), bf16[512,2560]{0,1:T(8,128)(2,1)}) %reduce-scatter.6.cloned.1.call-update) | async-done | bytes 2621456 | tf_op jit(solution)/shard_map/reduce_scatter | solution.py:181
  887.3 10.9 convolution_convert_fusion
  898.4 37.5 %reduce-scatter.12.cloned.1.call-done = bf16[640,1280]{1,0:T(8,128)(2,1)} async-done(((bf16[1280,1280]{1,0:T(8,128)(2,1)}), bf16[640,1280]{1,0:T(8,128)(2,1)}) %reduce-scatter.12.cloned.1.call-update) | async-done | bytes 1638416 | tf_op jit(solution)/shard_map/reduce_scatter | solution.py:202
  936.0 47.7 %reduce-scatter.14.cloned.1.call-done = bf16[640,1280]{1,0:T(8,128)(2,1)} async-done(((bf16[1280,1280]{1,0:T(8,128)(2,1)}), bf16[640,1280]{1,0:T(8,128)(2,1)}) %reduce-scatter.14.cloned.1.call-update) | async-done | bytes 1638416 | tf_op jit(solution)/shard_map/reduce_scatter | solution.py:205
  983.7 47.6 %reduce-scatter.10.cloned.1.call-done = bf16[640,1280]{1,0:T(8,128)(2,1)} async-done(((bf16[1280,1280]{1,0:T(8,128)(2,1)}), bf16[640,1280]{1,0:T(8,128)(2,1)}) %reduce-scatter.10.cloned.1.call-update) | async-done | bytes 1638416 | tf_op jit(solution)/shard_map/reduce_scatter | solution.py:199
  1031.3 117.7 %reduce-scatter.8.cloned.1.call-done = bf16[640,3840]{1,0:T(8,128)(2,1)} async-done(((bf16[1280,3840]{1,0:T(8,128)(2,1)}), bf16[640,3840]{1,0:T(8,128)(2,1)}) %reduce-scatter.8.cloned.1.call-update) | async-done | bytes 4915216 | tf_op jit(solution)/shard_map/reduce_scatter | solution.py:196
  1156.6 12.2 fusion.40
  1168.8 41.6 %all-reduce = (f32[1280]{0:T(1024)}, f32[1280]{0:T(1024)}, f32[80]{0:T(128)}) all-reduce(f32[1280]{0:T(1024)S(1)} %get-tuple-element.469, f32[1280]{0:T(1024)S(1)} %copy-done.24, f32[80]{0:T(128)S(1)} %divide_multiply_fusion), channel_id=1, replica_groups=mesh['grp'=4,'ctx'=4,'wt'=2] {'grp','ctx','wt'}, use_global_device_ids=true, to_apply=%region_21.22 | all-reduce | flops 2640 | bytes 21120 | tf_op jit(solution)/shard_map/psum | solution.py:215
  1214.8 131.1 %all-reduce.4.cloned.1.call-done = (bf16[640,3840]{1,0:T(8,128)(2,1)}, bf16[640,1280]{1,0:T(8,128)(2,1)}, bf16[640,1280]{1,0:T(8,128)(2,1)}, bf16[640,1280]{1,0:T(8,128)(2,1)}) async-done(((bf16[640,3840]{1,0:T(8,128)(2,1)}, bf16[640,1280]{1,0:T(8,128)(2,1)}, bf16[640,1280]{1,0:T(8,128)(2,1)}, bf16[640,1280]{1,0:T(8,128)(2,1)}), (bf16[640,3840]{1,0:T(8,128)(2,1)}, bf16[640,1280]{1,0:T(8,128)(2,1)}, ...) | async-done | bytes 9830416 | tf_op jit(solution)/shard_map/psum | solution.py:210
  (222 shorter events, 251.4 us)
Async XLA Ops:
  7.2 127.5 %copy-start.19 = (f32[1280]{0:T(1024)S(1)}, f32[1280]{0:T(1024)}, u32[]{:S(2)}) copy-start(f32[1280]{0:T(1024)} %param.20) | copy-start | bytes 15364
  7.2 127.4 %all-gather.6.cloned.1.call-start = ((), (), s32[]{:S(2)}) async-start(), calls=%async_computation.5 | async-start | bytes 14745600 | tf_op jit(solution)/shard_map/all_gather | solution.py:69
  7.9 323.5 %all-gather.8.cloned.1.call-start = ((), (), s32[]{:S(2)}) async-start(), calls=%async_computation.6 | async-start | bytes 13107200 | tf_op jit(solution)/shard_map/all_gather | solution.py:108
  9.4 132.9 %copy-start.22 = (f32[512]{0:T(512)}, f32[512]{0:T(512)S(1)}, u32[]{:S(2)}) copy-start(f32[512]{0:T(512)S(1)} %get-tuple-element.537) | copy-start | bytes 6148
  147.4 324.1 %all-gather.10.cloned.1.call-start = ((), (), s32[]{:S(2)}) async-start(), calls=%async_computation.7 | async-start | bytes 4915200 | tf_op jit(solution)/shard_map/all_gather | solution.py:70
  148.1 329.2 %all-gather.12.cloned.1.call-start = ((), (), s32[]{:S(2)}) async-start(), calls=%async_computation.8 | async-start | bytes 4915200 | tf_op jit(solution)/shard_map/all_gather | solution.py:71
  148.7 334.9 %all-gather.14.cloned.1.call-start = ((), (), s32[]{:S(2)}) async-start(), calls=%async_computation.9 | async-start | bytes 4915200 | tf_op jit(solution)/shard_map/all_gather | solution.py:72
  149.3 738.0 %reduce-scatter.6.cloned.1.call-start = ((), (), s32[]{:S(2)}) async-start(), calls=%async_computation.10 | async-start | bytes 13107200 | tf_op jit(solution)/shard_map/reduce_scatter | solution.py:181
  149.6 3.9 copy-start.29
  471.5 5.9 copy-start.25
  477.3 14.2 %copy-start.27 = (f32[512]{0:T(512)}, f32[512]{0:T(512)S(1)}, u32[]{:S(2)}) copy-start(f32[512]{0:T(512)S(1)} %get-tuple-element.539) | copy-start | bytes 6148
  477.3 6.3 copy-start.16
  483.6 5.1 copy-start.6
  483.6 5.1 copy-start.31
  550.2 6.2 copy-start.12
  597.5 6.3 copy-start.12
  644.9 6.2 copy-start.12
  692.2 6.2 copy-start.12
  710.9 225.1 %reduce-scatter.12.cloned.1.call-start = ((), (), s32[]{:S(2)}) async-start(), calls=%async_computation.13 | async-start | bytes 4915200 | tf_op jit(solution)/shard_map/reduce_scatter | solution.py:202
  717.6 266.1 %reduce-scatter.14.cloned.1.call-start = ((), (), s32[]{:S(2)}) async-start(), calls=%async_computation.14 | async-start | bytes 4915200 | tf_op jit(solution)/shard_map/reduce_scatter | solution.py:205
  724.4 307.0 %reduce-scatter.10.cloned.1.call-start = ((), (), s32[]{:S(2)}) async-start(), calls=%async_computation.12 | async-start | bytes 4915200 | tf_op jit(solution)/shard_map/reduce_scatter | solution.py:199
  731.0 418.0 %reduce-scatter.8.cloned.1.call-start = ((), (), s32[]{:S(2)}) async-start(), calls=%async_computation.11 | async-start | bytes 14745600 | tf_op jit(solution)/shard_map/reduce_scatter | solution.py:196
  732.7 154.6 %copy-start.20 = (f32[1280]{0:T(1024)S(1)}, f32[1280]{0:T(1024)}, u32[]{:S(2)}) copy-start(f32[1280]{0:T(1024)} %param.20) | copy-start | bytes 15364
  732.7 154.6 %copy-start.23 = (f32[512]{0:T(512)S(1)}, f32[512]{0:T(512)}, u32[]{:S(2)}) copy-start(f32[512]{0:T(512)} %copy-done.22) | copy-start | bytes 6148
  898.2 447.7 %all-reduce.4.cloned.1.call-start = ((), (), s32[]{:S(2)}) async-start(), calls=%async_computation.15 | async-start | bytes 19660800 | tf_op jit(solution)/shard_map/psum | solution.py:210
  1149.7 6.9 copy-start.4
  1149.7 6.9 copy-start.15
  1149.7 6.9 copy-start.32
  1156.6 12.2 copy-start.24
  1156.6 53.8 %copy-start.21 = (f32[512]{0:T(512)S(1)}, f32[512]{0:T(512)}, u32[]{:S(2)}) copy-start(f32[512]{0:T(512)} %get-tuple-element.536) | copy-start | bytes 6148
  1345.9 7.5 slice-start.1
  1349.4 3.9 slice-start.2
  (27 other events, 53.3 us)
Sparse Core Ops, SparseCore 0:
  9.6 125.0 all-gather.5
  147.5 183.9 all-gather.7
  333.0 44.5 all-gather.9
  379.0 46.4 all-gather.11
  426.9 46.3 all-gather.13
  711.0 176.2 reduce-scatter.5
  890.1 45.8 reduce-scatter.11
  938.9 44.7 reduce-scatter.13
  986.5 44.7 reduce-scatter.9
  1034.2 114.7 reduce-scatter.7
  1153.0 192.8 all-reduce.3
where the time goes:
time: 1370 us; the launch traced here: 1360 us
  waiting for transfers between devices  836 us (61%)
  matrix products  296 us (22%)
  other arithmetic  108 us (8%)
  local copies, waits for them, and re-layouts  67.2 us (5%)
  blocking collectives  41.6 us (3%)
  between operations  14.5 us (1%)
    all_gather x1, waiting for transfers between devices, local(): lax.all_gather(keyval, 'ctx', axis=0, tiled=True)  175 us
    reduce_scatter x1, waiting for transfers between devices, local(): lax.psum_scatter(grad_keyval.astype(jnp.bfloat16), 'ctx', scatter_dimensi...  151 us
    psum x1, waiting for transfers between devices, local(): lax.psum(shard_qkv.astype(jnp.bfloat16), ('grp', 'ctx')).astype(jnp.float32)  131 us
    all_gather x1, waiting for transfers between devices, local(): lax.all_gather(w_qkv, 'wt', axis=0, tiled=True)  125 us
    reduce_scatter x1, waiting for transfers between devices, local(): lax.psum_scatter(grad_w_qkv.astype(jnp.bfloat16), 'wt', scatter_dimension...  118 us
    reduce_scatter x1, waiting for transfers between devices, local(): lax.psum_scatter(grad_w_out.astype(jnp.bfloat16), 'wt', scatter_dimension...  47.7 us
    reduce_scatter x1, waiting for transfers between devices, local(): lax.psum_scatter(grad_w_proj.astype(jnp.bfloat16), 'wt', scatter_dimensio...  47.6 us
    dot_general x4, matrix products, backward_step(): jnp.einsum('hqk,qhd->khd', probs.astype(jnp.bfloat16), grad_attended, pre...  45.8 us
  transfers between devices with their start and end apart: 11, of which 8 were waited for; matrix products, arithmetic and copies ran while one was open for 15% of the time, Pallas kernels for 0%

commit v1 on v0

--- a/solution.py
+++ b/solution.py
@@ -1,3 +1,4 @@
+import functools
 import math
 import jax
 import jax.numpy as jnp
@@ -10,6 +11,15 @@
 epsilon = 1e-06
 scale_base = 1.442695041
 masked_fill = -1e30
+
+
+def hold_members_all_all(t0, axis_tag, group_axis):
+    return lax.psum(lax.psum(t0, axis_tag), group_axis)
+
+
+convert_the_figure = functools.partial(
+    hold_members_all_all, axis_tag="grp", group_axis=("ctx", "wt")
+)
 
 
 def rms_inverse(values):
@@ -212,8 +222,8 @@
         lax.psum(shard_in.astype(jnp.bfloat16), ("grp", "ctx")).astype(jnp.float32),
         lax.psum(shard_out.astype(jnp.bfloat16), ("grp", "ctx")).astype(jnp.float32),
     )
-    total_gain_attn, total_gain_mlp, total_scale = lax.psum(
-        (grad_gain_attn, grad_gain_mlp, grad_query_scale), ("grp", "ctx", "wt")
+    total_gain_attn, total_gain_mlp, total_scale = convert_the_figure(
+        (grad_gain_attn, grad_gain_mlp, grad_query_scale)
     )
     return (
         layer_out[None],

time: 1370 us -> 1370 us (level)
    psum x1 -> x2, blocking collectives: 41.6 us -> 50.6 us  [hold_members_all_all(): return lax.psum(lax.psum(t0, axis_tag), group_axis)]
where the time goes in v1:
time: 1370 us; the launch traced here: 1360 us
  waiting for transfers between devices  827 us (60%)
  matrix products  296 us (22%)
  other arithmetic  108 us (8%)
  local copies, waits for them, and re-layouts  67.2 us (5%)
  blocking collectives  50.6 us (4%)
  between operations  14.5 us (1%)
    all_gather x1, waiting for transfers between devices, local(): lax.all_gather(keyval, 'ctx', axis=0, tiled=True)  175 us
    reduce_scatter x1, waiting for transfers between devices, local(): lax.psum_scatter(grad_keyval.astype(jnp.bfloat16), 'ctx', scatter_dimensi...  151 us
    all_gather x1, waiting for transfers between devices, local(): lax.all_gather(w_qkv, 'wt', axis=0, tiled=True)  125 us
    psum x1, waiting for transfers between devices, local(): lax.psum(shard_qkv.astype(jnp.bfloat16), ('grp', 'ctx')).astype(jnp.float32)  122 us
    reduce_scatter x1, waiting for transfers between devices, local(): lax.psum_scatter(grad_w_qkv.astype(jnp.bfloat16), 'wt', scatter_dimension...  118 us
    psum x2, blocking collectives, hold_members_all_all(): return lax.psum(lax.psum(t0, axis_tag), group_axis)  50.6 us
    reduce_scatter x1, waiting for transfers between devices, local(): lax.psum_scatter(grad_w_out.astype(jnp.bfloat16), 'wt', scatter_dimension...  47.7 us
    reduce_scatter x1, waiting for transfers between devices, local(): lax.psum_scatter(grad_w_proj.astype(jnp.bfloat16), 'wt', scatter_dimensio...  47.6 us
  transfers between devices with their start and end apart: 11, of which 8 were waited for; matrix products, arithmetic and copies ran while one was open for 15% of the time, Pallas kernels for 0%

profile of v1, /device:TPU:0, one launch (start us, length us, event | category | flops | bytes accessed | tf_op | source)
XLA Modules:
  0.0 1364.5 jit_solution(1910236720841409726)
XLA Ops:
  9.4 125.2 %all-gather.6.cloned.1.call-done = bf16[1280,3840]{1,0:T(8,128)(2,1)} async-done(((bf16[640,3840]{1,0:T(8,128)(2,1)}), bf16[1280,3840]{1,0:T(8,128)(2,1)}) %all-gather.6.cloned.1.call-update) | async-done | bytes 9830416 | tf_op jit(solution)/shard_map/all_gather | solution.py:79
  156.0 175.5 %all-gather.8.cloned.1.call-done = bf16[2048,2560]{1,0:T(8,128)(2,1)} async-done(((bf16[512,2560]{1,0:T(8,128)(2,1)}), bf16[2048,2560]{1,0:T(8,128)(2,1)}) %all-gather.8.cloned.1.call-update) | async-done | bytes 10485776 | tf_op jit(solution)/shard_map/all_gather | solution.py:118
  331.5 14.7 %copy.34 = bf16[2048,2560]{0,1:T(8,128)(2,1)} copy(bf16[2048,2560]{1,0:T(8,128)(2,1)} %all-gather.8.cloned.1.call-done) | data formatting | bytes 20971520
  346.1 122.2 %while.34 = (s32[]{:T(128)}, f32[16,512]{1,0:T(8,128)S(1)}, f32[16,512]{1,0:T(8,128)S(1)}, f32[512,16,80]{0,2,1:T(8,128)}, s32[2048]{0:T(1024)S(1)}, /*index=5*/...) while((s32[]{:T(128)}, f32[16,512]{1,0:T(8,128)S(1)}, ...), condition=%wide.region_4.5_spmd.clone, body=%wide.region_1.4_spmd.clone.sunk | while | flops 1387185664 | bytes 66340068 | solution.py:64
  356.7 9.2 fusion.115
  365.9 9.7 bitcast_add_fusion.4
  386.9 9.9 fusion.115
  396.8 10.4 bitcast_add_fusion.4
  417.9 9.2 fusion.115
  427.1 10.8 bitcast_add_fusion.4
  457.6 10.4 bitcast_add_fusion.4
  500.8 9.7 broadcast_in_dim.141
  510.5 188.1 %while.35 = (s32[]{:T(128)}, f32[512,16,80]{0,2,1:T(8,128)}, f32[2048,2560]{0,1:T(8,128)}, bf16[2048,2560]{0,1:T(8,128)(2,1)}, s32[2048]{0:T(1024)S(1)}, /*index...) while((s32[]{:T(128)}, f32[512,16,80]{0,2,1:T(8,128)}, ...), condition=%wide.region_9.10_spmd.clone, body=%wide.region_8.9_spmd.clone.sunk | while | flops 3402368512 | bytes 138003792 | solution.py:64
  523.5 11.4 fusion.130
  534.9 9.7 fusion.129
  569.1 11.4 fusion.130
  580.5 9.7 fusion.129
  616.4 11.4 fusion.130
  627.8 9.7 fusion.129
  663.7 11.4 fusion.130
  675.2 9.7 fusion.129
  698.6 12.3 convert_element_type.118
  736.3 151.1 %reduce-scatter.6.cloned.1.call-done = bf16[512,2560]{0,1:T(8,128)(2,1)} async-done(((bf16[2048,2560]{0,1:T(8,128)(2,1)}), bf16[512,2560]{0,1:T(8,128)(2,1)}) %reduce-scatter.6.cloned.1.call-update) | async-done | bytes 2621456 | tf_op jit(solution)/shard_map/reduce_scatter | solution.py:191
  887.4 10.9 convolution_convert_fusion
  898.5 37.5 %reduce-scatter.12.cloned.1.call-done = bf16[640,1280]{1,0:T(8,128)(2,1)} async-done(((bf16[1280,1280]{1,0:T(8,128)(2,1)}), bf16[640,1280]{1,0:T(8,128)(2,1)}) %reduce-scatter.12.cloned.1.call-update) | async-done | bytes 1638416 | tf_op jit(solution)/shard_map/reduce_scatter | solution.py:212
  936.0 47.7 %reduce-scatter.14.cloned.1.call-done = bf16[640,1280]{1,0:T(8,128)(2,1)} async-done(((bf16[1280,1280]{1,0:T(8,128)(2,1)}), bf16[640,1280]{1,0:T(8,128)(2,1)}) %reduce-scatter.14.cloned.1.call-update) | async-done | bytes 1638416 | tf_op jit(solution)/shard_map/reduce_scatter | solution.py:215
  983.8 47.6 %reduce-scatter.10.cloned.1.call-done = bf16[640,1280]{1,0:T(8,128)(2,1)} async-done(((bf16[1280,1280]{1,0:T(8,128)(2,1)}), bf16[640,1280]{1,0:T(8,128)(2,1)}) %reduce-scatter.10.cloned.1.call-update) | async-done | bytes 1638416 | tf_op jit(solution)/shard_map/reduce_scatter | solution.py:209
  1031.4 117.7 %reduce-scatter.8.cloned.1.call-done = bf16[640,3840]{1,0:T(8,128)(2,1)} async-done(((bf16[1280,3840]{1,0:T(8,128)(2,1)}), bf16[640,3840]{1,0:T(8,128)(2,1)}) %reduce-scatter.8.cloned.1.call-update) | async-done | bytes 4915216 | tf_op jit(solution)/shard_map/reduce_scatter | solution.py:206
  1156.7 12.2 fusion.40
  1168.9 12.5 all-reduce.1
  1181.3 38.2 %all-reduce = (f32[1280]{0:T(1024)}, f32[1280]{0:T(1024)}, f32[80]{0:T(128)}) all-reduce(f32[1280]{0:T(1024)S(1)} %get-tuple-element.514, f32[1280]{0:T(1024)S(1)} %get-tuple-element.515, f32[80]{0:T(128)S(1)} %get-tuple-element.516), channel_id=1, replica_groups=mesh['grp'=4,'ctx'=4,'wt'=2] {'ctx','wt'}, use_global_device_ids=true, to_apply=%region_22.23 | all-reduce | flops 2640 | bytes 21120 | tf_op jit(solution)/shard_map/psum | solution.py:17
  1223.8 121.8 %all-reduce.5.cloned.1.call-done = (bf16[640,3840]{1,0:T(8,128)(2,1)}, bf16[640,1280]{1,0:T(8,128)(2,1)}, bf16[640,1280]{1,0:T(8,128)(2,1)}, bf16[640,1280]{1,0:T(8,128)(2,1)}) async-done(((bf16[640,3840]{1,0:T(8,128)(2,1)}, bf16[640,1280]{1,0:T(8,128)(2,1)}, bf16[640,1280]{1,0:T(8,128)(2,1)}, bf16[640,1280]{1,0:T(8,128)(2,1)}), (bf16[640,3840]{1,0:T(8,128)(2,1)}, bf16[640,1280]{1,0:T(8,128)(2,1)}, ...) | async-done | bytes 9830416 | tf_op jit(solution)/shard_map/psum | solution.py:220
  (223 shorter events, 260.5 us)
Async XLA Ops:
  7.2 127.5 %copy-start.19 = (f32[1280]{0:T(1024)S(1)}, f32[1280]{0:T(1024)}, u32[]{:S(2)}) copy-start(f32[1280]{0:T(1024)} %param.20) | copy-start | bytes 15364
  7.2 127.4 %all-gather.6.cloned.1.call-start = ((), (), s32[]{:S(2)}) async-start(), calls=%async_computation.5 | async-start | bytes 14745600 | tf_op jit(solution)/shard_map/all_gather | solution.py:79
  7.9 323.5 %all-gather.8.cloned.1.call-start = ((), (), s32[]{:S(2)}) async-start(), calls=%async_computation.6 | async-start | bytes 13107200 | tf_op jit(solution)/shard_map/all_gather | solution.py:118
  9.4 132.9 %copy-start.22 = (f32[512]{0:T(512)}, f32[512]{0:T(512)S(1)}, u32[]{:S(2)}) copy-start(f32[512]{0:T(512)S(1)} %get-tuple-element.540) | copy-start | bytes 6148
  147.4 324.2 %all-gather.10.cloned.1.call-start = ((), (), s32[]{:S(2)}) async-start(), calls=%async_computation.7 | async-start | bytes 4915200 | tf_op jit(solution)/shard_map/all_gather | solution.py:80
  148.1 329.3 %all-gather.12.cloned.1.call-start = ((), (), s32[]{:S(2)}) async-start(), calls=%async_computation.8 | async-start | bytes 4915200 | tf_op jit(solution)/shard_map/all_gather | solution.py:81
  148.7 335.0 %all-gather.14.cloned.1.call-start = ((), (), s32[]{:S(2)}) async-start(), calls=%async_computation.9 | async-start | bytes 4915200 | tf_op jit(solution)/shard_map/all_gather | solution.py:82
  149.3 738.1 %reduce-scatter.6.cloned.1.call-start = ((), (), s32[]{:S(2)}) async-start(), calls=%async_computation.10 | async-start | bytes 13107200 | tf_op jit(solution)/shard_map/reduce_scatter | solution.py:191
  149.6 3.9 copy-start.29
  471.6 5.9 copy-start.25
  477.4 14.2 %copy-start.27 = (f32[512]{0:T(512)}, f32[512]{0:T(512)S(1)}, u32[]{:S(2)}) copy-start(f32[512]{0:T(512)S(1)} %get-tuple-element.542) | copy-start | bytes 6148
  477.5 6.3 copy-start.16
  483.8 5.1 copy-start.8
  483.8 5.1 copy-start.31
  550.3 6.2 copy-start.12
  597.6 6.2 copy-start.12
  644.9 6.2 copy-start.12
  692.2 6.3 copy-start.12
  710.9 225.1 %reduce-scatter.12.cloned.1.call-start = ((), (), s32[]{:S(2)}) async-start(), calls=%async_computation.13 | async-start | bytes 4915200 | tf_op jit(solution)/shard_map/reduce_scatter | solution.py:212
  717.7 266.1 %reduce-scatter.14.cloned.1.call-start = ((), (), s32[]{:S(2)}) async-start(), calls=%async_computation.14 | async-start | bytes 4915200 | tf_op jit(solution)/shard_map/reduce_scatter | solution.py:215
  724.4 307.0 %reduce-scatter.10.cloned.1.call-start = ((), (), s32[]{:S(2)}) async-start(), calls=%async_computation.12 | async-start | bytes 4915200 | tf_op jit(solution)/shard_map/reduce_scatter | solution.py:209
  731.1 418.0 %reduce-scatter.8.cloned.1.call-start = ((), (), s32[]{:S(2)}) async-start(), calls=%async_computation.11 | async-start | bytes 14745600 | tf_op jit(solution)/shard_map/reduce_scatter | solution.py:206
  732.8 154.6 %copy-start.20 = (f32[1280]{0:T(1024)S(1)}, f32[1280]{0:T(1024)}, u32[]{:S(2)}) copy-start(f32[1280]{0:T(1024)} %param.20) | copy-start | bytes 15364
  732.8 154.6 %copy-start.23 = (f32[512]{0:T(512)S(1)}, f32[512]{0:T(512)}, u32[]{:S(2)}) copy-start(f32[512]{0:T(512)} %copy-done.22) | copy-start | bytes 6148
  898.3 447.4 %all-reduce.5.cloned.1.call-start = ((), (), s32[]{:S(2)}) async-start(), calls=%async_computation.15 | async-start | bytes 19660800 | tf_op jit(solution)/shard_map/psum | solution.py:220
  1149.8 6.9 copy-start.4
  1149.8 6.9 copy-start.15
  1149.8 6.9 copy-start.32
  1156.7 12.2 copy-start.24
  1156.7 62.8 %copy-start.21 = (f32[512]{0:T(512)S(1)}, f32[512]{0:T(512)}, u32[]{:S(2)}) copy-start(f32[512]{0:T(512)} %get-tuple-element.539) | copy-start | bytes 6148
  1345.6 7.5 slice-start.1
  1349.2 3.9 slice-start.2
  (27 other events, 53.3 us)
Sparse Core Ops, SparseCore 0:
  9.6 125.0 all-gather.5
  147.5 183.9 all-gather.7
  333.0 44.5 all-gather.9
  379.0 46.4 all-gather.11
  426.9 46.4 all-gather.13
  711.1 176.2 reduce-scatter.5
  890.2 45.8 reduce-scatter.11
  939.0 44.7 reduce-scatter.13
  986.6 44.7 reduce-scatter.9
  1034.3 114.7 reduce-scatter.7
  1153.1 192.5 all-reduce.4
